TPU v7x, 32 devices: a whole 2x2x4 slice. The times are simulated.
32 devices in a mesh: dp: 8 (over z, y), tensor: 4 (over x, core).
Axes of the slice: x: 2, y: 2, z: 4, core: 2. Of those that a mesh axis runs over, the one named last changes fastest.
Arguments:
- block_in: float32 [4096, 640], P(('dp', 'tensor')), may hold values from -6 to 6
- d_output: float32 [4096, 640], P(('dp', 'tensor')), may hold values from -6 to 6
- doc_ids: int32 [8, 512], P('dp'), may hold values from 0 to 3, never falling along the last dimension, each value on 1 to 256 neighbouring positions
- w_query: float32 [640, 1024], P('dp', 'tensor'), may hold values from -0.25 to 0.25
- w_key: float32 [640, 256], P('dp'), may hold values from -0.25 to 0.25
- w_value: float32 [640, 256], P('dp'), may hold values from -0.25 to 0.25
- w_output: float32 [640, 1024], P('dp', 'tensor'), may hold values from -0.1875 to 0.1875
- w_gate: float32 [640, 2048], P('dp', 'tensor'), may hold values from -0.25 to 0.25
- w_up: float32 [640, 2048], P('dp', 'tensor'), may hold values from -0.25 to 0.25
- w_down: float32 [640, 2048], P('dp', 'tensor'), may hold values from -0.125 to 0.125
- mom_query: float32 [640, 1024], P('dp', 'tensor'), may hold values from -112 to 112
- mom_key: float32 [640, 256], P('dp'), may hold values from -112 to 112
- mom_value: float32 [640, 256], P('dp'), may hold values from -112 to 112
- mom_output: float32 [640, 1024], P('dp', 'tensor'), may hold values from -112 to 112
- mom_gate: float32 [640, 2048], P('dp', 'tensor'), may hold values from -112 to 112
- mom_up: float32 [640, 2048], P('dp', 'tensor'), may hold values from -112 to 112
- mom_down: float32 [640, 2048], P('dp', 'tensor'), may hold values from -112 to 112
- gains: float32 [3072], replicated, may hold values from -0.4 to 0.6
- adam_first: float32 [3072], replicated, may hold values from -112 to 112
- adam_second: float32 [3072], replicated, may hold values from 204.8 to 8192
Outputs:
- block_out: float32 [4096, 640], P(('dp', 'tensor'))
- d_input: float32 [4096, 640], P(('dp', 'tensor'))
- grad_query: float32 [640, 1024], P('dp', 'tensor')
- grad_key: float32 [640, 256], P('dp')
- grad_value: float32 [640, 256], P('dp')
- grad_output: float32 [640, 1024], P('dp', 'tensor')
- grad_gate: float32 [640, 2048], P('dp', 'tensor')
- grad_up: float32 [640, 2048], P('dp', 'tensor')
- grad_down: float32 [640, 2048], P('dp', 'tensor')
- grad_gains: float32 [3072], replicated
- new_query: float32 [640, 1024], P('dp', 'tensor')
- new_key: float32 [640, 256], P('dp')
- new_value: float32 [640, 256], P('dp')
- new_output: float32 [640, 1024], P('dp', 'tensor')
- new_gate: float32 [640, 2048], P('dp', 'tensor')
- new_up: float32 [640, 2048], P('dp', 'tensor')
- new_down: float32 [640, 2048], P('dp', 'tensor')
- momentum_query: float32 [640, 1024], P('dp', 'tensor')
- momentum_key: float32 [640, 256], P('dp')
- momentum_value: float32 [640, 256], P('dp')
- momentum_output: float32 [640, 1024], P('dp', 'tensor')
- momentum_gate: float32 [640, 2048], P('dp', 'tensor')
- momentum_up: float32 [640, 2048], P('dp', 'tensor')
- momentum_down: float32 [640, 2048], P('dp', 'tensor')
- new_gains: float32 [3072], replicated
- next_first: float32 [3072], replicated
- next_second: float32 [3072], replicated
Inputs may be any that keep to these rules, and one draw needn't show every extreme that they name: `doc_ids`: along each sequence the document id never falls; each document covers 1 to half of 512 tokens, and some document covers exactly half of 512.
All inputs are finite; a program needn't handle non-finite values.
Results may differ from a plain program's by a relative error of at most 0.02.
Values may be sent and summed in bfloat16 or wider, within the bound.
No kernel may reach another device: no remote copies, remote signals or barrier semaphores. Data moves between devices by JAX's collectives and lax.ppermute only.
A program may use at most 64 MiB of HBM per device.

v0:
```python
import math
import jax
import jax.numpy as jnp
from jax import lax
from jax.sharding import PartitionSpec as P

NS_STEPS = 5
STEP = 5
EPSILON = 1e-06
ROPE_BASE = 10000.0
MUON_BETA = 0.95
MUON_RATE = 0.04
MUON_DECAY = 0.1
POLY_FIRST = 3.4445
POLY_SECOND = -4.775
POLY_THIRD = 2.0315
FIRST_DECAY = 0.9
SECOND_DECAY = 0.95
ADAM_RATE = 0.05
ADAM_EPSILON = 1e-08
MASKED = -1e30


def rms_norm(values, gain):
    factor = lax.rsqrt(jnp.mean(values * values, axis=-1, keepdims=True) + EPSILON)
    return values * factor * (1.0 + gain)


def rotate(values, cosine, sine):
    half = values.shape[-1] // 2
    turned = jnp.concatenate([-values[..., half:], values[..., :half]], axis=-1)
    return values * cosine + turned * sine


def head_map(raw, gain, cosine, sine):
    return rotate(rms_norm(raw, gain), cosine, sine)


def gated(gate, upper):
    return jax.nn.gelu(gate, approximate=True) * upper


def rope_tables(doc_rows, head_width):
    length = doc_rows.shape[-1]
    first = jnp.sum((doc_rows[..., None, :] < doc_rows[..., :, None]).astype(jnp.int32), axis=-1)
    offset = (jnp.arange(length, dtype=jnp.int32) - first).astype(jnp.float32)
    freqs = ROPE_BASE ** (-(2.0 * jnp.arange(head_width // 2, dtype=jnp.float32)) / head_width)
    angles = offset[..., None] * freqs
    angles = jnp.concatenate([angles, angles], axis=-1)
    return (jnp.cos(angles), jnp.sin(angles))


def gather_rows(values):
    return lax.all_gather(values, "tensor", axis=0, tiled=True)


def sum_rows(term, rows):
    return lax.psum_scatter(
        term(jnp.int32(0), rows * lax.axis_size("tensor")).astype(jnp.bfloat16),
        "tensor",
        scatter_dimension=0,
        tiled=True,
    ).astype(jnp.float32)


def gram_whole(matrix, share):
    gram_part = jnp.dot(matrix, matrix.T, preferred_element_type=jnp.float32) * share
    gram_rows = lax.psum_scatter(
        gram_part.astype(jnp.bfloat16), "tensor", scatter_dimension=0, tiled=True
    )
    return lax.all_gather(gram_rows, "tensor", axis=0, tiled=True)


def poly_step(ortho, square):
    once = jnp.dot(square, ortho, preferred_element_type=jnp.float32).astype(jnp.bfloat16)
    twice = jnp.dot(square, once, preferred_element_type=jnp.float32)
    mixed = (
        POLY_FIRST * ortho.astype(jnp.float32)
        + POLY_SECOND * once.astype(jnp.float32)
        + POLY_THIRD * twice
    )
    return mixed.astype(jnp.bfloat16)


def body(
    block_in,
    d_output,
    doc_ids,
    w_query,
    w_key,
    w_value,
    w_output,
    w_gate,
    w_up,
    w_down,
    mom_query,
    mom_key,
    mom_value,
    mom_output,
    mom_gate,
    mom_up,
    mom_down,
    gains,
    adam_first,
    adam_second,
):
    f32 = jnp.float32
    bf16 = jnp.bfloat16
    tensor_count = lax.axis_size("tensor")
    data_count = lax.axis_size("dp")
    local_rows = block_in.shape[0]
    model_width = block_in.shape[1]
    head_width = w_key.shape[1]
    local_heads = w_query.shape[1] // head_width
    seq_count = doc_ids.shape[0]
    seq_len = doc_ids.shape[1]
    total_rows = seq_count * seq_len
    scale = head_width ** (-0.5)
    pre_attn = gains[0:model_width]
    post_attn = gains[model_width : 2 * model_width]
    pre_ffn = gains[2 * model_width : 3 * model_width]
    post_ffn = gains[3 * model_width : 4 * model_width]
    gain_q = gains[4 * model_width : 4 * model_width + head_width]
    gain_k = gains[4 * model_width + head_width :]
    full_query, full_key, full_value, full_output, full_gate, full_up, full_down = (
        lax.all_gather(w_query.astype(bf16), "dp", axis=0, tiled=True),
        lax.all_gather(w_key.astype(bf16), "dp", axis=0, tiled=True),
        lax.all_gather(w_value.astype(bf16), "dp", axis=0, tiled=True),
        lax.all_gather(w_output.astype(bf16), "dp", axis=0, tiled=True),
        lax.all_gather(w_gate.astype(bf16), "dp", axis=0, tiled=True),
        lax.all_gather(w_up.astype(bf16), "dp", axis=0, tiled=True),
        lax.all_gather(w_down.astype(bf16), "dp", axis=0, tiled=True),
    )
    cosine, sine = rope_tables(doc_ids, head_width)
    places = jnp.arange(seq_len)
    allowed = (doc_ids[:, None, :] == doc_ids[:, :, None]) & (places[None, :] <= places[:, None])[
        None
    ]
    normed_one = gather_rows(rms_norm(block_in, pre_attn).astype(bf16))
    queries = jnp.dot(normed_one, full_query, preferred_element_type=f32).reshape(
        seq_count, seq_len, local_heads, head_width
    )
    keys = jnp.dot(normed_one, full_key, preferred_element_type=f32).reshape(
        seq_count, seq_len, head_width
    )
    values = (
        jnp.dot(normed_one, full_value, preferred_element_type=f32)
        .astype(bf16)
        .reshape(seq_count, seq_len, head_width)
    )
    query_rot = head_map(queries, gain_q, cosine[:, :, None, :], sine[:, :, None, :]).astype(bf16)
    key_rot = head_map(keys, gain_k, cosine, sine).astype(bf16)

    def masked_scores():
        raw = jnp.einsum("bshd,btd->bhst", query_rot, key_rot, preferred_element_type=f32) * scale
        return jnp.where(allowed[:, None], raw, MASKED)

    scores = masked_scores()
    top = jnp.max(scores, axis=-1, keepdims=True)
    log_total = top + jnp.log(jnp.sum(jnp.exp(scores - top), axis=-1, keepdims=True))
    probs = jnp.exp(scores - log_total).astype(bf16)
    heads = jnp.einsum("bhst,btd->bshd", probs, values, preferred_element_type=f32).astype(bf16)
    heads_flat = heads.reshape(total_rows, local_heads * head_width)

    def attn_term(start, count):
        return jnp.dot(heads_flat, full_output.T, preferred_element_type=f32)

    attn_local = sum_rows(attn_term, local_rows)
    middle = block_in + rms_norm(attn_local, post_attn)
    normed_two = gather_rows(rms_norm(middle, pre_ffn).astype(bf16))
    gate = jnp.dot(normed_two, full_gate, preferred_element_type=f32)
    upper = jnp.dot(normed_two, full_up, preferred_element_type=f32)
    hidden = gated(gate, upper).astype(bf16)

    def branch_term(start, count):
        return jnp.dot(hidden, full_down.T, preferred_element_type=f32)

    branch_local = sum_rows(branch_term, local_rows)
    block_out = middle + rms_norm(branch_local, post_ffn)
    pull = jax.vjp(rms_norm, branch_local, post_ffn)[1]
    d_branch_local, g_post_ffn = pull(d_output)
    branch_low = gather_rows(d_branch_local.astype(bf16))
    grad_down_part = jnp.einsum("rd,rf->df", branch_low, hidden, preferred_element_type=f32)
    d_hidden = jnp.dot(branch_low, full_down, preferred_element_type=f32)
    pull = jax.vjp(gated, gate, upper)[1]
    d_gate, d_upper = pull(d_hidden)
    gate_low = d_gate.astype(bf16)
    upper_low = d_upper.astype(bf16)
    grad_gate_part = jnp.einsum("rd,rf->df", normed_two, gate_low, preferred_element_type=f32)
    grad_up_part = jnp.einsum("rd,rf->df", normed_two, upper_low, preferred_element_type=f32)

    def hidden_term(start, count):
        first_part = jnp.dot(gate_low, full_gate.T, preferred_element_type=f32)
        return first_part + jnp.dot(upper_low, full_up.T, preferred_element_type=f32)

    d_normed_two = sum_rows(hidden_term, local_rows)
    pull = jax.vjp(rms_norm, middle, pre_ffn)[1]
    d_mid_extra, g_pre_ffn = pull(d_normed_two)
    d_middle = d_output + d_mid_extra
    pull = jax.vjp(rms_norm, attn_local, post_attn)[1]
    d_attn_local, g_post_attn = pull(d_middle)
    attn_low = gather_rows(d_attn_local.astype(bf16))
    grad_output_part = jnp.einsum("rd,re->de", attn_low, heads_flat, preferred_element_type=f32)
    d_heads = jnp.dot(attn_low, full_output, preferred_element_type=f32).astype(bf16)
    d_heads = d_heads.reshape(seq_count, seq_len, local_heads, head_width)
    prob_full = jnp.exp(masked_scores() - log_total)
    delta = jnp.einsum("bshd,bshd->bhs", d_heads, heads, preferred_element_type=f32)
    d_probs = jnp.einsum("bshd,btd->bhst", d_heads, values, preferred_element_type=f32)
    d_scores = (prob_full * (d_probs - delta[..., None]) * scale).astype(bf16)
    d_qrot = jnp.einsum("bhst,btd->bshd", d_scores, key_rot, preferred_element_type=f32)
    d_krot = jnp.einsum("bhst,bshd->bthd", d_scores, query_rot, preferred_element_type=f32)
    d_vals = jnp.einsum("bhst,bshd->bthd", probs, d_heads, preferred_element_type=f32)
    pull = jax.vjp(
        lambda raw, gain: head_map(raw, gain, cosine[:, :, None, :], sine[:, :, None, :]),
        queries,
        gain_q,
    )[1]
    d_queries, g_query = pull(d_qrot)
    pull = jax.vjp(lambda raw, gain: head_map(raw, gain, cosine, sine), keys, gain_k)[1]
    d_keys, g_key_heads = jax.vmap(pull, in_axes=2, out_axes=(2, 0))(d_krot)
    g_key = jnp.sum(g_key_heads, axis=0)
    query_low = d_queries.reshape(total_rows, local_heads * head_width).astype(bf16)
    key_low = d_keys.reshape(total_rows, local_heads, head_width).astype(bf16)
    value_low = d_vals.reshape(total_rows, local_heads, head_width).astype(bf16)
    grad_query_part = jnp.einsum("rd,re->de", normed_one, query_low, preferred_element_type=f32)
    grad_key_part = jnp.einsum("rd,rhe->de", normed_one, key_low, preferred_element_type=f32)
    grad_value_part = jnp.einsum("rd,rhe->de", normed_one, value_low, preferred_element_type=f32)

    def query_term(start, count):
        first_part = jnp.dot(query_low, full_query.T, preferred_element_type=f32)
        second_part = jnp.einsum("rhe,de->rd", key_low, full_key, preferred_element_type=f32)
        third_part = jnp.einsum("rhe,de->rd", value_low, full_value, preferred_element_type=f32)
        return first_part + second_part + third_part

    d_normed_one = sum_rows(query_term, local_rows)
    pull = jax.vjp(rms_norm, block_in, pre_attn)[1]
    d_in_extra, g_pre_attn = pull(d_normed_one)
    d_input = d_middle + d_in_extra
    gain_term = jnp.concatenate([g_pre_attn, g_post_attn, g_pre_ffn, g_post_ffn, g_query, g_key])
    sum_query, sum_output, sum_gate, sum_up, sum_down = (
        lax.psum_scatter(grad_query_part, "dp", scatter_dimension=0, tiled=True),
        lax.psum_scatter(grad_output_part, "dp", scatter_dimension=0, tiled=True),
        lax.psum_scatter(grad_gate_part, "dp", scatter_dimension=0, tiled=True),
        lax.psum_scatter(grad_up_part, "dp", scatter_dimension=0, tiled=True),
        lax.psum_scatter(grad_down_part, "dp", scatter_dimension=0, tiled=True),
    )
    key_total, value_total, grad_gains = lax.psum(
        (grad_key_part, grad_value_part, gain_term), ("dp", "tensor")
    )
    shard_rows = w_key.shape[0]
    my_data = lax.axis_index("dp")
    sum_key = lax.dynamic_slice_in_dim(key_total, my_data * shard_rows, shard_rows, 0)
    sum_value = lax.dynamic_slice_in_dim(value_total, my_data * shard_rows, shard_rows, 0)
    weights = (w_query, w_key, w_value, w_output, w_gate, w_up, w_down)
    moments = (mom_query, mom_key, mom_value, mom_output, mom_gate, mom_up, mom_down)
    reduced = (sum_query, sum_key, sum_value, sum_output, sum_gate, sum_up, sum_down)
    whole_cols = [
        weights[index].shape[1] * (1 if index in (1, 2) else tensor_count) for index in range(7)
    ]
    slot = max([weight.shape[1] for weight in weights])
    owners = [index * data_count // 7 for index in range(7)]
    moved = [MUON_BETA * moments[index] + reduced[index] for index in range(7)]
    outgoing = jnp.zeros((data_count, shard_rows, slot), bf16)
    for index in range(7):
        push = (reduced[index] + MUON_BETA * moved[index]).astype(bf16)
        padded = jnp.pad(push, ((0, 0), (0, slot - push.shape[1])))
        outgoing = outgoing.at[owners[index]].set(padded)
    arrived = lax.all_to_all(outgoing, "dp", split_axis=0, concat_axis=0, tiled=True)
    owned = arrived.reshape(data_count * shard_rows, slot)
    shared = (my_data == owners[1]) | (my_data == owners[2])
    share = jnp.where(shared, 1.0 / tensor_count, 1.0).astype(f32)
    owned_wide = owned.astype(f32)
    raw_square = gram_whole(owned, share)
    norm_total = jnp.sum(jnp.diagonal(raw_square).astype(f32))
    ortho = (owned_wide / (jnp.sqrt(norm_total) + 1e-07)).astype(bf16)
    for index in range(NS_STEPS):
        square = gram_whole(ortho, share)
        ortho = poly_step(ortho, square)
    returned = lax.all_to_all(
        ortho.reshape(data_count, shard_rows, slot), "dp", split_axis=0, concat_axis=0, tiled=True
    )
    updated = []
    for index in range(7):
        weight = weights[index]
        update = returned[owners[index], :, : weight.shape[1]].astype(f32)
        factor = 0.2 * math.sqrt(max(model_width, whole_cols[index]))
        updated.append(weight - MUON_RATE * (factor * update + MUON_DECAY * weight))
    next_first = FIRST_DECAY * adam_first + (1.0 - FIRST_DECAY) * grad_gains
    next_second = SECOND_DECAY * adam_second + (1.0 - SECOND_DECAY) * grad_gains * grad_gains
    first_fix = 1.0 - FIRST_DECAY**STEP
    second_fix = 1.0 - SECOND_DECAY**STEP
    new_gains = gains - ADAM_RATE * (next_first / first_fix) / (
        jnp.sqrt(next_second / second_fix) + ADAM_EPSILON
    )
    return (
        block_out,
        d_input,
        sum_query,
        sum_key,
        sum_value,
        sum_output,
        sum_gate,
        sum_up,
        sum_down,
        grad_gains,
        updated[0],
        updated[1],
        updated[2],
        updated[3],
        updated[4],
        updated[5],
        updated[6],
        moved[0],
        moved[1],
        moved[2],
        moved[3],
        moved[4],
        moved[5],
        moved[6],
        new_gains,
        next_first,
        next_second,
    )


def solution(mesh):
    return jax.shard_map(
        body,
        mesh=mesh,
        in_specs=(
            P(("dp", "tensor"), None),
            P(("dp", "tensor"), None),
            P("dp", None),
            P("dp", "tensor"),
            P("dp", None),
            P("dp", None),
            P("dp", "tensor"),
            P("dp", "tensor"),
            P("dp", "tensor"),
            P("dp", "tensor"),
            P("dp", "tensor"),
            P("dp", None),
            P("dp", None),
            P("dp", "tensor"),
            P("dp", "tensor"),
            P("dp", "tensor"),
            P("dp", "tensor"),
            P(),
            P(),
            P(),
        ),
        out_specs=(
            P(("dp", "tensor"), None),
            P(("dp", "tensor"), None),
            P("dp", "tensor"),
            P("dp", None),
            P("dp", None),
            P("dp", "tensor"),
            P("dp", "tensor"),
            P("dp", "tensor"),
            P("dp", "tensor"),
            P(),
            P("dp", "tensor"),
            P("dp", None),
            P("dp", None),
            P("dp", "tensor"),
            P("dp", "tensor"),
            P("dp", "tensor"),
            P("dp", "tensor"),
            P("dp", "tensor"),
            P("dp", None),
            P("dp", None),
            P("dp", "tensor"),
            P("dp", "tensor"),
            P("dp", "tensor"),
            P("dp", "tensor"),
            P(),
            P(),
            P(),
        ),
        check_vma=False,
    )
```

profile of v0, /device:TPU:0, one launch (start us, length us, event | category | flops | bytes accessed | tf_op | source)
XLA Modules:
  0.0 1146.8 jit_solution(16319865074403344235)
XLA Ops:
  11.0 9.4 all_gather.51
  20.4 31.4 %all_gather.53 = bf16[640,256]{1,0:T(8,128)(2,1)S(1)} all-gather(bf16[80,256]{1,0:T(8,128)(2,1)S(1)} %convert_element_type.303), channel_id=1, replica_groups=mesh['dp'=8,'tensor'=4] {'dp'}, dimensions={0}, use_global_device_ids=true | all-gather | bytes 368640 | tf_op jit(solution)/shard_map/all_gather | solution.py:127
  53.1 30.8 %all_gather.54 = bf16[640,256]{1,0:T(8,128)(2,1)S(1)} all-gather(bf16[80,256]{1,0:T(8,128)(2,1)S(1)} %convert_element_type.307), channel_id=1, replica_groups=mesh['dp'=8,'tensor'=4] {'dp'}, dimensions={0}, use_global_device_ids=true | all-gather | bytes 368640 | tf_op jit(solution)/shard_map/all_gather | solution.py:126
  89.8 31.0 %all_gather.52 = bf16[640,256]{1,0:T(8,128)(2,1)S(1)} all-gather(bf16[80,256]{1,0:T(8,128)(2,1)S(1)} %convert_element_type.301), channel_id=1, replica_groups=mesh['dp'=8,'tensor'=4] {'dp'}, dimensions={0}, use_global_device_ids=true | all-gather | bytes 368640 | tf_op jit(solution)/shard_map/all_gather | solution.py:128
  121.5 31.3 %all_gather.55 = bf16[640,256]{1,0:T(8,128)(2,1)S(1)} all-gather(bf16[80,256]{1,0:T(8,128)(2,1)S(1)} %convert_element_type.313), channel_id=1, replica_groups=mesh['dp'=8,'tensor'=4] {'dp'}, dimensions={0}, use_global_device_ids=true | all-gather | bytes 368640 | tf_op jit(solution)/shard_map/all_gather | solution.py:129
  157.4 34.0 %all_gather.57 = bf16[640,512]{1,0:T(8,128)(2,1)} all-gather(bf16[80,512]{1,0:T(8,128)(2,1)S(1)} %convert_element_type.317), channel_id=1, replica_groups=mesh['dp'=8,'tensor'=4] {'dp'}, dimensions={0}, use_global_device_ids=true | all-gather | bytes 737280 | tf_op jit(solution)/shard_map/all_gather | solution.py:130
  191.3 33.8 %all_gather.58 = bf16[640,512]{1,0:T(8,128)(2,1)} all-gather(bf16[80,512]{1,0:T(8,128)(2,1)S(1)} %convert_element_type.318), channel_id=1, replica_groups=mesh['dp'=8,'tensor'=4] {'dp'}, dimensions={0}, use_global_device_ids=true | all-gather | bytes 737280 | tf_op jit(solution)/shard_map/all_gather | solution.py:131
  225.1 33.4 %all_gather.59 = bf16[640,512]{1,0:T(8,128)(2,1)} all-gather(bf16[80,512]{1,0:T(8,128)(2,1)S(1)} %convert_element_type.320), channel_id=1, replica_groups=mesh['dp'=8,'tensor'=4] {'dp'}, dimensions={0}, use_global_device_ids=true | all-gather | bytes 737280 | tf_op jit(solution)/shard_map/all_gather | solution.py:132
  274.1 23.2 %reduce-scatter.18.cloned.1.call-done = bf16[128,640]{1,0:T(8,128)(2,1)} async-done(((bf16[512,640]{1,0:T(8,128)(2,1)}), bf16[128,640]{1,0:T(8,128)(2,1)}) %reduce-scatter.18.cloned.1.call-update) | async-done | bytes 163856 | tf_op jit(solution)/shard_map/reduce_scatter | solution.py:58
  313.9 23.1 %reduce-scatter.20.cloned.1.call-done = bf16[128,640]{1,0:T(8,128)(2,1)} async-done(((bf16[512,640]{1,0:T(8,128)(2,1)}), bf16[128,640]{1,0:T(8,128)(2,1)}) %reduce-scatter.20.cloned.1.call-update) | async-done | bytes 163856 | tf_op jit(solution)/shard_map/reduce_scatter | solution.py:58
  342.0 7.5 all_gather.61
  379.7 120.8 %all-reduce.12.cloned.1.call-done = (f32[640,256]{1,0:T(8,128)}, f32[640,256]{1,0:T(8,128)}) async-done(((f32[640,256]{1,0:T(8,128)}, f32[640,256]{1,0:T(8,128)}), (f32[640,256]{1,0:T(8,128)}, f32[640,256]{1,0:T(8,128)})) %all-reduce.12.cloned.1.call-update) | async-done | bytes 1310736 | tf_op jit(solution)/shard_map/psum | solution.py:247
  502.2 63.7 %reduce-scatter.24.cloned.1.call-done = f32[80,256]{1,0:T(8,128)} async-done(((f32[640,256]{1,0:T(8,128)}), f32[80,256]{1,0:T(8,128)}) %reduce-scatter.24.cloned.1.call-update) | async-done | bytes 81936 | tf_op jit(solution)/shard_map/reduce_scatter | solution.py:241
  569.7 61.8 %reduce-scatter.26.cloned.1.call-done = f32[80,256]{1,0:T(8,128)} async-done(((f32[640,256]{1,0:T(8,128)}), f32[80,256]{1,0:T(8,128)}) %reduce-scatter.26.cloned.1.call-update) | async-done | bytes 81936 | tf_op jit(solution)/shard_map/reduce_scatter | solution.py:242
  633.6 65.9 %reduce-scatter.28.cloned.1.call-done = f32[80,512]{1,0:T(8,128)} async-done(((f32[640,512]{1,0:T(8,128)}), f32[80,512]{1,0:T(8,128)}) %reduce-scatter.28.cloned.1.call-update) | async-done | bytes 163856 | tf_op jit(solution)/shard_map/reduce_scatter | solution.py:243
  701.2 66.3 %reduce-scatter.30.cloned.1.call-done = f32[80,512]{1,0:T(8,128)} async-done(((f32[640,512]{1,0:T(8,128)}), f32[80,512]{1,0:T(8,128)}) %reduce-scatter.30.cloned.1.call-update) | async-done | bytes 163856 | tf_op jit(solution)/shard_map/reduce_scatter | solution.py:244
  769.2 66.4 %reduce-scatter.32.cloned.1.call-done = f32[80,512]{1,0:T(8,128)} async-done(((f32[640,512]{1,0:T(8,128)}), f32[80,512]{1,0:T(8,128)}) %reduce-scatter.32.cloned.1.call-update) | async-done | bytes 163856 | tf_op jit(solution)/shard_map/reduce_scatter | solution.py:245
  840.9 15.5 %all-to-all-done = bf16[8,80,512]{2,1,0:T(8,128)(2,1)S(1)} async-done(((bf16[8,80,512]{2,1,0:T(8,128)(2,1)}), bf16[8,80,512]{2,1,0:T(8,128)(2,1)S(1)}, u32[]{:S(2)}, u32[]{:S(2)}) %all-to-all-start) | async-done | bytes 655392 | tf_op jit(solution)/shard_map/all_to_all | solution.py:268
  858.0 22.6 %reduce-scatter.34.cloned.1.call-done = bf16[160,640]{1,0:T(8,128)(2,1)} async-done(((bf16[640,640]{1,0:T(8,128)(2,1)}), bf16[160,640]{1,0:T(8,128)(2,1)}) %reduce-scatter.34.cloned.1.call-update) | async-done | bytes 204816 | tf_op jit(solution)/shard_map/reduce_scatter | solution.py:68
  880.6 8.4 all_gather.62
  898.0 23.9 %reduce-scatter.36.cloned.1.call-done = bf16[160,640]{1,0:T(8,128)(2,1)} async-done(((bf16[640,640]{1,0:T(8,128)(2,1)}), bf16[160,640]{1,0:T(8,128)(2,1)}) %reduce-scatter.36.cloned.1.call-update) | async-done | bytes 204816 | tf_op jit(solution)/shard_map/reduce_scatter | solution.py:68
  921.9 8.6 all_gather.63
  933.6 24.1 %reduce-scatter.38.cloned.1.call-done = bf16[160,640]{1,0:T(8,128)(2,1)} async-done(((bf16[640,640]{1,0:T(8,128)(2,1)}), bf16[160,640]{1,0:T(8,128)(2,1)}) %reduce-scatter.38.cloned.1.call-update) | async-done | bytes 204816 | tf_op jit(solution)/shard_map/reduce_scatter | solution.py:68
  957.7 8.4 all_gather.64
  969.2 24.1 %reduce-scatter.40.cloned.1.call-done = bf16[160,640]{1,0:T(8,128)(2,1)} async-done(((bf16[640,640]{1,0:T(8,128)(2,1)}), bf16[160,640]{1,0:T(8,128)(2,1)}) %reduce-scatter.40.cloned.1.call-update) | async-done | bytes 204816 | tf_op jit(solution)/shard_map/reduce_scatter | solution.py:68
  993.3 8.4 all_gather.65
  1008.1 20.8 %reduce-scatter.42.cloned.1.call-done = bf16[160,640]{1,0:T(8,128)(2,1)} async-done(((bf16[640,640]{1,0:T(8,128)(2,1)}), bf16[160,640]{1,0:T(8,128)(2,1)}) %reduce-scatter.42.cloned.1.call-update) | async-done | bytes 204816 | tf_op jit(solution)/shard_map/reduce_scatter | solution.py:68
  1028.9 8.4 all_gather.66
  1040.4 13.3 %reduce-scatter.22.cloned.1.call-done = bf16[128,640]{1,0:T(8,128)(2,1)} async-done(((bf16[512,640]{1,0:T(8,128)(2,1)}), bf16[128,640]{1,0:T(8,128)(2,1)}) %reduce-scatter.22.cloned.1.call-update) | async-done | bytes 163856 | tf_op jit(solution)/shard_map/reduce_scatter | solution.py:58
  1054.8 24.8 %reduce-scatter.44.cloned.1.call-done = bf16[160,640]{1,0:T(8,128)(2,1)} async-done(((bf16[640,640]{1,0:T(8,128)(2,1)}), bf16[160,640]{1,0:T(8,128)(2,1)}) %reduce-scatter.44.cloned.1.call-update) | async-done | bytes 204816 | tf_op jit(solution)/shard_map/reduce_scatter | solution.py:68
  1079.6 8.4 all_gather.67
  1096.1 41.0 %psum.23 = f32[3072]{0:T(1024)S(1)} all-reduce(f32[3072]{0:T(1024)S(1)} %constant_dynamic-update-slice_fusion), channel_id=1, replica_groups=mesh['dp'=8,'tensor'=4] {'dp','tensor'}, use_global_device_ids=true, to_apply=%region_32.33 | all-reduce | flops 3072 | bytes 24576 | tf_op jit(solution)/shard_map/psum | solution.py:247
  (318 shorter events, 136.8 us)
Async XLA Ops:
  7.2 251.3 %reduce-scatter.16.cloned.1.call-start = ((), (), s32[]{:S(2)}) async-start(), calls=%async_computation.17 | async-start | bytes 819200 | tf_op jit(solution)/shard_map/reduce_scatter | solution.py:58
  154.5 142.8 %reduce-scatter.18.cloned.1.call-start = ((), (), s32[]{:S(2)}) async-start(), calls=%async_computation.18 | async-start | bytes 819200 | tf_op jit(solution)/shard_map/reduce_scatter | solution.py:58
  156.4 103.2 %copy-start = (f32[128,640]{1,0:T(8,128)S(1)}, f32[128,640]{1,0:T(8,128)}, u32[]{:S(2)}) copy-start(f32[128,640]{1,0:T(8,128)} %param.34) | copy-start | bytes 983044
  260.8 76.2 %copy-start.72 = (f32[128]{0:T(128)}, f32[128]{0:T(128)S(1)}, u32[]{:S(2)}) copy-start(f32[128]{0:T(128)S(1)} %fusion.115) | copy-start | bytes 1540
  274.0 62.9 %reduce-scatter.20.cloned.1.call-start = ((), (), s32[]{:S(2)}) async-start(), calls=%async_computation.19 | async-start | bytes 819200 | tf_op jit(solution)/shard_map/reduce_scatter | solution.py:58
  313.8 186.7 %all-reduce.12.cloned.1.call-start = ((), (), s32[]{:S(2)}) async-start(), calls=%async_computation.32 | async-start | bytes 2621440 | tf_op jit(solution)/shard_map/psum | solution.py:247
  367.7 198.2 %reduce-scatter.24.cloned.1.call-start = ((), (), s32[]{:S(2)}) async-start(), calls=%async_computation.21 | async-start | bytes 737280 | tf_op jit(solution)/shard_map/reduce_scatter | solution.py:241
  373.1 258.3 %reduce-scatter.26.cloned.1.call-start = ((), (), s32[]{:S(2)}) async-start(), calls=%async_computation.22 | async-start | bytes 737280 | tf_op jit(solution)/shard_map/reduce_scatter | solution.py:242
  374.5 325.1 %reduce-scatter.28.cloned.1.call-start = ((), (), s32[]{:S(2)}) async-start(), calls=%async_computation.23 | async-start | bytes 1474560 | tf_op jit(solution)/shard_map/reduce_scatter | solution.py:243
  376.3 391.2 %reduce-scatter.30.cloned.1.call-start = ((), (), s32[]{:S(2)}) async-start(), calls=%async_computation.24 | async-start | bytes 1474560 | tf_op jit(solution)/shard_map/reduce_scatter | solution.py:244
  378.0 122.6 %copy-start.63 = (f32[80,256]{1,0:T(8,128)S(1)}, f32[80,256]{1,0:T(8,128)}, u32[]{:S(2)}) copy-start(f32[80,256]{1,0:T(8,128)} %param.46) | copy-start | bytes 245764
  378.0 122.6 %copy-start.64 = (f32[80,256]{1,0:T(8,128)S(1)}, f32[80,256]{1,0:T(8,128)}, u32[]{:S(2)}) copy-start(f32[80,256]{1,0:T(8,128)} %param.45) | copy-start | bytes 245764
  378.0 457.6 %reduce-scatter.32.cloned.1.call-start = ((), (), s32[]{:S(2)}) async-start(), calls=%async_computation.25 | async-start | bytes 1474560 | tf_op jit(solution)/shard_map/reduce_scatter | solution.py:245
  379.7 186.3 %copy-start.65 = (f32[80,256]{1,0:T(8,128)S(1)}, f32[80,256]{1,0:T(8,128)}, u32[]{:S(2)}) copy-start(f32[80,256]{1,0:T(8,128)} %param.44) | copy-start | bytes 245764
  379.7 251.8 %copy-start.66 = (f32[80,256]{1,0:T(8,128)S(1)}, f32[80,256]{1,0:T(8,128)}, u32[]{:S(2)}) copy-start(f32[80,256]{1,0:T(8,128)} %param.47) | copy-start | bytes 245764
  379.7 319.9 %copy-start.60 = (f32[80,512]{1,0:T(8,128)S(1)}, f32[80,512]{1,0:T(8,128)}, u32[]{:S(2)}) copy-start(f32[80,512]{1,0:T(8,128)} %param.48) | copy-start | bytes 491524
  502.2 265.3 %copy-start.61 = (f32[80,512]{1,0:T(8,128)S(1)}, f32[80,512]{1,0:T(8,128)}, u32[]{:S(2)}) copy-start(f32[80,512]{1,0:T(8,128)} %param.49) | copy-start | bytes 491524
  567.5 268.1 %copy-start.62 = (f32[80,512]{1,0:T(8,128)S(1)}, f32[80,512]{1,0:T(8,128)}, u32[]{:S(2)}) copy-start(f32[80,512]{1,0:T(8,128)} %param.50) | copy-start | bytes 491524
  837.2 19.1 %all-to-all-start = ((bf16[8,80,512]{2,1,0:T(8,128)(2,1)}), bf16[8,80,512]{2,1,0:T(8,128)(2,1)S(1)}, u32[]{:S(2)}, u32[]{:S(2)}) async-start(bf16[8,80,512]{2,1,0:T(8,128)(2,1)} %get-tuple-element.128), calls=%async_computation.9 | async-start | bytes 1310720 | tf_op jit(solution)/shard_map/all_to_all | solution.py:268
  840.8 39.8 %reduce-scatter.34.cloned.1.call-start = ((), (), s32[]{:S(2)}) async-start(), calls=%async_computation.26 | async-start | bytes 1024000 | tf_op jit(solution)/shard_map/reduce_scatter | solution.py:68
  858.0 64.0 %reduce-scatter.36.cloned.1.call-start = ((), (), s32[]{:S(2)}) async-start(), calls=%async_computation.27 | async-start | bytes 1024000 | tf_op jit(solution)/shard_map/reduce_scatter | solution.py:68
  897.8 59.9 %reduce-scatter.38.cloned.1.call-start = ((), (), s32[]{:S(2)}) async-start(), calls=%async_computation.28 | async-start | bytes 1024000 | tf_op jit(solution)/shard_map/reduce_scatter | solution.py:68
  933.6 59.7 %reduce-scatter.40.cloned.1.call-start = ((), (), s32[]{:S(2)}) async-start(), calls=%async_computation.29 | async-start | bytes 1024000 | tf_op jit(solution)/shard_map/reduce_scatter | solution.py:68
  969.2 59.7 %reduce-scatter.42.cloned.1.call-start = ((), (), s32[]{:S(2)}) async-start(), calls=%async_computation.30 | async-start | bytes 1024000 | tf_op jit(solution)/shard_map/reduce_scatter | solution.py:68
  1004.8 48.9 %reduce-scatter.22.cloned.1.call-start = ((), (), s32[]{:S(2)}) async-start(), calls=%async_computation.20 | async-start | bytes 819200 | tf_op jit(solution)/shard_map/reduce_scatter | solution.py:58
  1008.1 71.5 %reduce-scatter.44.cloned.1.call-start = ((), (), s32[]{:S(2)}) async-start(), calls=%async_computation.31 | async-start | bytes 1024000 | tf_op jit(solution)/shard_map/reduce_scatter | solution.py:68
  1090.3 47.5 %copy-start.15 = (f32[128,640]{1,0:T(8,128)S(1)}, f32[128,640]{1,0:T(8,128)}, u32[]{:S(2)}) copy-start(f32[128,640]{1,0:T(8,128)} %copy-done.14) | copy-start | bytes 983044
  1090.3 47.5 %copy-start.50 = (bf16[128,640]{1,0:T(8,128)(2,1)S(1)}, bf16[128,640]{1,0:T(8,128)(2,1)}, u32[]{:S(2)}) copy-start(bf16[128,640]{1,0:T(8,128)(2,1)} %reduce-scatter.22.cloned.1.call-done) | copy-start | bytes 491524
  1090.3 48.3 %copy-start.47 = (f32[80,512]{1,0:T(8,128)S(1)}, f32[80,512]{1,0:T(8,128)}, u32[]{:S(2)}) copy-start(f32[80,512]{1,0:T(8,128)} %param.41) | copy-start | bytes 491524
  1090.3 48.3 %copy-start.48 = (f32[80,512]{1,0:T(8,128)S(1)}, f32[80,512]{1,0:T(8,128)}, u32[]{:S(2)}) copy-start(f32[80,512]{1,0:T(8,128)} %param.42) | copy-start | bytes 491524
  1090.3 48.3 %copy-start.49 = (f32[80,512]{1,0:T(8,128)S(1)}, f32[80,512]{1,0:T(8,128)}, u32[]{:S(2)}) copy-start(f32[80,512]{1,0:T(8,128)} %param.43) | copy-start | bytes 491524
  1090.4 48.3 %all-to-all-start.1 = ((bf16[8,80,512]{2,1,0:T(8,128)(2,1)}), bf16[8,80,512]{2,1,0:T(8,128)(2,1)S(1)}, u32[]{:S(2)}, u32[]{:S(2)}) async-start(bf16[8,80,512]{2,1,0:T(8,128)(2,1)} %bitcast.48), calls=%async_computation.16 | async-start | bytes 1310720 | tf_op jit(solution)/shard_map/all_to_all | solution.py:279
  (65 other events, 600.7 us)
Sparse Core Ops, SparseCore 0:
  154.6 22.7 reduce-scatter.15
  274.2 23.0 reduce-scatter.17
  313.9 22.9 reduce-scatter.19
  367.8 132.6 all-reduce.11
  504.2 61.6 reduce-scatter.23
  569.6 61.7 reduce-scatter.25
  635.4 64.1 reduce-scatter.27
  703.5 63.9 reduce-scatter.29
  771.5 64.0 reduce-scatter.31
  858.1 22.4 reduce-scatter.33
  897.9 23.9 reduce-scatter.35
  933.7 23.9 reduce-scatter.37
  969.3 23.9 reduce-scatter.39
  1004.9 23.9 reduce-scatter.41
  1031.3 22.3 reduce-scatter.21
  1056.1 23.4 reduce-scatter.43
where the time goes:
time: 1150 us
  waiting for transfers between devices  661 us (57%)
  blocking collectives  349 us (30%)
  matrix products  49.4 us (4%)
  other arithmetic  43.5 us (4%)
  local copies, waits for them, and re-layouts  19 us (2%)
  between operations  15.7 us (1%)
    reduce_scatter x6, waiting for transfers between devices, gram_whole(): lax.psum_scatter(gram_part.astype(jnp.bfloat16), 'tensor', scatter_dimens...  140 us
    psum x1, waiting for transfers between devices, body(): lax.psum((grad_key_part, grad_value_part, gain_term), ('dp', 'tensor'))  121 us
    reduce_scatter x1, waiting for transfers between devices, body(): lax.psum_scatter(grad_down_part, 'dp', scatter_dimension=0, tiled=True)  66.4 us
    reduce_scatter x1, waiting for transfers between devices, body(): lax.psum_scatter(grad_up_part, 'dp', scatter_dimension=0, tiled=True)  66.3 us
    reduce_scatter x1, waiting for transfers between devices, body(): lax.psum_scatter(grad_gate_part, 'dp', scatter_dimension=0, tiled=True)  65.9 us
    reduce_scatter x1, waiting for transfers between devices, body(): lax.psum_scatter(grad_query_part, 'dp', scatter_dimension=0, tiled=True)  63.7 us
    reduce_scatter x1, waiting for transfers between devices, body(): lax.psum_scatter(grad_output_part, 'dp', scatter_dimension=0, tiled=True)  61.8 us
    reduce_scatter x4, waiting for transfers between devices, sum_rows(): lax.psum_scatter(term(jnp.int32(0), rows * lax.axis_size('tensor')).astyp...  59.6 us
  transfers between devices with their start and end apart: 18, of which 16 were waited for; matrix products, arithmetic and copies ran while one was open for 3% of the time, Pallas kernels for 0%

commit v1 on v0

--- a/solution.py
+++ b/solution.py
@@ -19,6 +19,11 @@
 ADAM_RATE = 0.05
 ADAM_EPSILON = 1e-08
 MASKED = -1e30
+
+
+def axis_by_axis(x, one, other):
+    partial = lax.psum(x, one)
+    return lax.psum(partial, other)
 
 
 def rms_norm(values, gain):
@@ -244,8 +249,8 @@
         lax.psum_scatter(grad_up_part, "dp", scatter_dimension=0, tiled=True),
         lax.psum_scatter(grad_down_part, "dp", scatter_dimension=0, tiled=True),
     )
-    key_total, value_total, grad_gains = lax.psum(
-        (grad_key_part, grad_value_part, gain_term), ("dp", "tensor")
+    key_total, value_total, grad_gains = axis_by_axis(
+        (grad_key_part, grad_value_part, gain_term), "tensor", "dp"
     )
     shard_rows = w_key.shape[0]
     my_data = lax.axis_index("dp")

time: 1150 us -> 1150 us (level)
    psum x1 -> x2, blocking collectives: 41 us -> 48.7 us  [the longest x1 37.4 us: axis_by_axis(): return lax.psum(partial, other)]
    psum x1 -> x2, waiting for transfers between devices: 121 us -> 118 us  [the longest x1 84.9 us: axis_by_axis(): return lax.psum(partial, other)]
  transfers between devices with their start and end apart: 18 -> 19, of which waited for: 16 -> 17; matrix products, arithmetic and copies ran while one was open for 3% -> 3% of each run, Pallas kernels for 0% -> 0%
where the time goes in v1:
time: 1150 us
  waiting for transfers between devices  655 us (57%)
  blocking collectives  357 us (31%)
  matrix products  49.4 us (4%)
  other arithmetic  43.5 us (4%)
  local copies, waits for them, and re-layouts  19 us (2%)
  between operations  15.7 us (1%)
    reduce_scatter x6, waiting for transfers between devices, gram_whole(): lax.psum_scatter(gram_part.astype(jnp.bfloat16), 'tensor', scatter_dimens...  140 us
    psum x1, waiting for transfers between devices, axis_by_axis(): return lax.psum(partial, other)  84.9 us
    reduce_scatter x1, waiting for transfers between devices, body(): lax.psum_scatter(grad_up_part, 'dp', scatter_dimension=0, tiled=True)  66.6 us
    reduce_scatter x1, waiting for transfers between devices, body(): lax.psum_scatter(grad_down_part, 'dp', scatter_dimension=0, tiled=True)  66.4 us
    reduce_scatter x1, waiting for transfers between devices, body(): lax.psum_scatter(grad_gate_part, 'dp', scatter_dimension=0, tiled=True)  64.6 us
    reduce_scatter x1, waiting for transfers between devices, body(): lax.psum_scatter(grad_output_part, 'dp', scatter_dimension=0, tiled=True)  63 us
    reduce_scatter x1, waiting for transfers between devices, body(): lax.psum_scatter(grad_query_part, 'dp', scatter_dimension=0, tiled=True)  61.3 us
    reduce_scatter x4, waiting for transfers between devices, sum_rows(): lax.psum_scatter(term(jnp.int32(0), rows * lax.axis_size('tensor')).astyp...  59.4 us
  transfers between devices with their start and end apart: 19, of which 17 were waited for; matrix products, arithmetic and copies ran while one was open for 3% of the time, Pallas kernels for 0%

profile of v1, /device:TPU:0, one launch (start us, length us, event | category | flops | bytes accessed | tf_op | source)
XLA Modules:
  0.0 1149.2 jit_solution(7139461176965732375)
XLA Ops:
  11.0 9.4 all_gather.51
  20.4 31.4 %all_gather.53 = bf16[640,256]{1,0:T(8,128)(2,1)S(1)} all-gather(bf16[80,256]{1,0:T(8,128)(2,1)S(1)} %convert_element_type.303), channel_id=1, replica_groups=mesh['dp'=8,'tensor'=4] {'dp'}, dimensions={0}, use_global_device_ids=true | all-gather | bytes 368640 | tf_op jit(solution)/shard_map/all_gather | solution.py:132
  53.1 30.8 %all_gather.54 = bf16[640,256]{1,0:T(8,128)(2,1)S(1)} all-gather(bf16[80,256]{1,0:T(8,128)(2,1)S(1)} %convert_element_type.307), channel_id=1, replica_groups=mesh['dp'=8,'tensor'=4] {'dp'}, dimensions={0}, use_global_device_ids=true | all-gather | bytes 368640 | tf_op jit(solution)/shard_map/all_gather | solution.py:131
  89.8 31.0 %all_gather.52 = bf16[640,256]{1,0:T(8,128)(2,1)S(1)} all-gather(bf16[80,256]{1,0:T(8,128)(2,1)S(1)} %convert_element_type.301), channel_id=1, replica_groups=mesh['dp'=8,'tensor'=4] {'dp'}, dimensions={0}, use_global_device_ids=true | all-gather | bytes 368640 | tf_op jit(solution)/shard_map/all_gather | solution.py:133
  121.6 31.3 %all_gather.55 = bf16[640,256]{1,0:T(8,128)(2,1)S(1)} all-gather(bf16[80,256]{1,0:T(8,128)(2,1)S(1)} %convert_element_type.313), channel_id=1, replica_groups=mesh['dp'=8,'tensor'=4] {'dp'}, dimensions={0}, use_global_device_ids=true | all-gather | bytes 368640 | tf_op jit(solution)/shard_map/all_gather | solution.py:134
  157.4 34.0 %all_gather.57 = bf16[640,512]{1,0:T(8,128)(2,1)} all-gather(bf16[80,512]{1,0:T(8,128)(2,1)S(1)} %convert_element_type.317), channel_id=1, replica_groups=mesh['dp'=8,'tensor'=4] {'dp'}, dimensions={0}, use_global_device_ids=true | all-gather | bytes 737280 | tf_op jit(solution)/shard_map/all_gather | solution.py:135
  191.4 33.7 %all_gather.58 = bf16[640,512]{1,0:T(8,128)(2,1)} all-gather(bf16[80,512]{1,0:T(8,128)(2,1)S(1)} %convert_element_type.318), channel_id=1, replica_groups=mesh['dp'=8,'tensor'=4] {'dp'}, dimensions={0}, use_global_device_ids=true | all-gather | bytes 737280 | tf_op jit(solution)/shard_map/all_gather | solution.py:136
  225.1 33.4 %all_gather.59 = bf16[640,512]{1,0:T(8,128)(2,1)} all-gather(bf16[80,512]{1,0:T(8,128)(2,1)S(1)} %convert_element_type.320), channel_id=1, replica_groups=mesh['dp'=8,'tensor'=4] {'dp'}, dimensions={0}, use_global_device_ids=true | all-gather | bytes 737280 | tf_op jit(solution)/shard_map/all_gather | solution.py:137
  274.3 23.0 %reduce-scatter.18.cloned.1.call-done = bf16[128,640]{1,0:T(8,128)(2,1)} async-done(((bf16[512,640]{1,0:T(8,128)(2,1)}), bf16[128,640]{1,0:T(8,128)(2,1)}) %reduce-scatter.18.cloned.1.call-update) | async-done | bytes 163856 | tf_op jit(solution)/shard_map/reduce_scatter | solution.py:63
  313.9 23.1 %reduce-scatter.20.cloned.1.call-done = bf16[128,640]{1,0:T(8,128)(2,1)} async-done(((bf16[512,640]{1,0:T(8,128)(2,1)}), bf16[128,640]{1,0:T(8,128)(2,1)}) %reduce-scatter.20.cloned.1.call-update) | async-done | bytes 163856 | tf_op jit(solution)/shard_map/reduce_scatter | solution.py:63
  374.6 33.0 %all-reduce.16.cloned.1.call-done = (f32[640,256]{1,0:T(8,128)}, f32[640,256]{1,0:T(8,128)}) async-done(((f32[640,256]{1,0:T(8,128)}, f32[640,256]{1,0:T(8,128)}), (f32[640,256]{1,0:T(8,128)}, f32[640,256]{1,0:T(8,128)})) %all-reduce.16.cloned.1.call-update) | async-done | bytes 1310736 | tf_op jit(solution)/shard_map/psum | solution.py:25
  412.8 61.3 %reduce-scatter.24.cloned.1.call-done = f32[80,256]{1,0:T(8,128)} async-done(((f32[640,256]{1,0:T(8,128)}), f32[80,256]{1,0:T(8,128)}) %reduce-scatter.24.cloned.1.call-update) | async-done | bytes 81936 | tf_op jit(solution)/shard_map/reduce_scatter | solution.py:246
  476.5 63.0 %reduce-scatter.26.cloned.1.call-done = f32[80,256]{1,0:T(8,128)} async-done(((f32[640,256]{1,0:T(8,128)}), f32[80,256]{1,0:T(8,128)}) %reduce-scatter.26.cloned.1.call-update) | async-done | bytes 81936 | tf_op jit(solution)/shard_map/reduce_scatter | solution.py:247
  541.1 84.9 %all-reduce.14.cloned.1.call-done = (f32[640,256]{1,0:T(8,128)}, f32[640,256]{1,0:T(8,128)}) async-done(((f32[640,256]{1,0:T(8,128)}, f32[640,256]{1,0:T(8,128)}), (f32[640,256]{1,0:T(8,128)}, f32[640,256]{1,0:T(8,128)})) %all-reduce.14.cloned.1.call-update) | async-done | bytes 1310736 | tf_op jit(solution)/shard_map/psum | solution.py:26
  629.5 64.6 %reduce-scatter.28.cloned.1.call-done = f32[80,512]{1,0:T(8,128)} async-done(((f32[640,512]{1,0:T(8,128)}), f32[80,512]{1,0:T(8,128)}) %reduce-scatter.28.cloned.1.call-update) | async-done | bytes 163856 | tf_op jit(solution)/shard_map/reduce_scatter | solution.py:248
  695.7 66.6 %reduce-scatter.30.cloned.1.call-done = f32[80,512]{1,0:T(8,128)} async-done(((f32[640,512]{1,0:T(8,128)}), f32[80,512]{1,0:T(8,128)}) %reduce-scatter.30.cloned.1.call-update) | async-done | bytes 163856 | tf_op jit(solution)/shard_map/reduce_scatter | solution.py:249
  763.9 66.4 %reduce-scatter.32.cloned.1.call-done = f32[80,512]{1,0:T(8,128)} async-done(((f32[640,512]{1,0:T(8,128)}), f32[80,512]{1,0:T(8,128)}) %reduce-scatter.32.cloned.1.call-update) | async-done | bytes 163856 | tf_op jit(solution)/shard_map/reduce_scatter | solution.py:250
  835.6 15.5 %all-to-all-done = bf16[8,80,512]{2,1,0:T(8,128)(2,1)S(1)} async-done(((bf16[8,80,512]{2,1,0:T(8,128)(2,1)}), bf16[8,80,512]{2,1,0:T(8,128)(2,1)S(1)}, u32[]{:S(2)}, u32[]{:S(2)}) %all-to-all-start) | async-done | bytes 655392 | tf_op jit(solution)/shard_map/all_to_all | solution.py:273
  852.8 22.5 %reduce-scatter.34.cloned.1.call-done = bf16[160,640]{1,0:T(8,128)(2,1)} async-done(((bf16[640,640]{1,0:T(8,128)(2,1)}), bf16[160,640]{1,0:T(8,128)(2,1)}) %reduce-scatter.34.cloned.1.call-update) | async-done | bytes 204816 | tf_op jit(solution)/shard_map/reduce_scatter | solution.py:73
  875.3 8.4 all_gather.62
  892.7 23.9 %reduce-scatter.36.cloned.1.call-done = bf16[160,640]{1,0:T(8,128)(2,1)} async-done(((bf16[640,640]{1,0:T(8,128)(2,1)}), bf16[160,640]{1,0:T(8,128)(2,1)}) %reduce-scatter.36.cloned.1.call-update) | async-done | bytes 204816 | tf_op jit(solution)/shard_map/reduce_scatter | solution.py:73
  916.6 8.6 all_gather.63
  928.4 24.0 %reduce-scatter.38.cloned.1.call-done = bf16[160,640]{1,0:T(8,128)(2,1)} async-done(((bf16[640,640]{1,0:T(8,128)(2,1)}), bf16[160,640]{1,0:T(8,128)(2,1)}) %reduce-scatter.38.cloned.1.call-update) | async-done | bytes 204816 | tf_op jit(solution)/shard_map/reduce_scatter | solution.py:73
  952.4 8.4 all_gather.64
  963.9 24.1 %reduce-scatter.40.cloned.1.call-done = bf16[160,640]{1,0:T(8,128)(2,1)} async-done(((bf16[640,640]{1,0:T(8,128)(2,1)}), bf16[160,640]{1,0:T(8,128)(2,1)}) %reduce-scatter.40.cloned.1.call-update) | async-done | bytes 204816 | tf_op jit(solution)/shard_map/reduce_scatter | solution.py:73
  1002.9 20.8 %reduce-scatter.42.cloned.1.call-done = bf16[160,640]{1,0:T(8,128)(2,1)} async-done(((bf16[640,640]{1,0:T(8,128)(2,1)}), bf16[160,640]{1,0:T(8,128)(2,1)}) %reduce-scatter.42.cloned.1.call-update) | async-done | bytes 204816 | tf_op jit(solution)/shard_map/reduce_scatter | solution.py:73
  1023.6 8.4 all_gather.66
  1035.1 13.3 %reduce-scatter.22.cloned.1.call-done = bf16[128,640]{1,0:T(8,128)(2,1)} async-done(((bf16[512,640]{1,0:T(8,128)(2,1)}), bf16[128,640]{1,0:T(8,128)(2,1)}) %reduce-scatter.22.cloned.1.call-update) | async-done | bytes 163856 | tf_op jit(solution)/shard_map/reduce_scatter | solution.py:63
  1049.5 24.8 %reduce-scatter.44.cloned.1.call-done = bf16[160,640]{1,0:T(8,128)(2,1)} async-done(((bf16[640,640]{1,0:T(8,128)(2,1)}), bf16[160,640]{1,0:T(8,128)(2,1)}) %reduce-scatter.44.cloned.1.call-update) | async-done | bytes 204816 | tf_op jit(solution)/shard_map/reduce_scatter | solution.py:73
  1074.3 8.4 all_gather.67
  1090.8 11.3 psum.46
  1102.1 37.4 %psum.47 = f32[3072]{0:T(1024)S(1)} all-reduce(f32[3072]{0:T(1024)S(1)} %psum.46), channel_id=1, replica_groups=mesh['dp'=8,'tensor'=4] {'dp'}, use_global_device_ids=true, to_apply=%region_35.36 | all-reduce | flops 3072 | bytes 24576 | tf_op jit(solution)/shard_map/psum | solution.py:26
  (322 shorter events, 152.9 us)
Async XLA Ops:
  7.2 251.3 %reduce-scatter.16.cloned.1.call-start = ((), (), s32[]{:S(2)}) async-start(), calls=%async_computation.17 | async-start | bytes 819200 | tf_op jit(solution)/shard_map/reduce_scatter | solution.py:63
  154.5 142.8 %reduce-scatter.18.cloned.1.call-start = ((), (), s32[]{:S(2)}) async-start(), calls=%async_computation.18 | async-start | bytes 819200 | tf_op jit(solution)/shard_map/reduce_scatter | solution.py:63
  156.4 103.2 %copy-start = (f32[128,640]{1,0:T(8,128)S(1)}, f32[128,640]{1,0:T(8,128)}, u32[]{:S(2)}) copy-start(f32[128,640]{1,0:T(8,128)} %param.34) | copy-start | bytes 983044
  260.8 76.2 %copy-start.72 = (f32[128]{0:T(128)}, f32[128]{0:T(128)S(1)}, u32[]{:S(2)}) copy-start(f32[128]{0:T(128)S(1)} %fusion.115) | copy-start | bytes 1540
  274.2 62.8 %reduce-scatter.20.cloned.1.call-start = ((), (), s32[]{:S(2)}) async-start(), calls=%async_computation.19 | async-start | bytes 819200 | tf_op jit(solution)/shard_map/reduce_scatter | solution.py:63
  313.8 93.8 %all-reduce.16.cloned.1.call-start = ((), (), s32[]{:S(2)}) async-start(), calls=%async_computation.33 | async-start | bytes 2621440 | tf_op jit(solution)/shard_map/psum | solution.py:25
  367.8 106.3 %reduce-scatter.24.cloned.1.call-start = ((), (), s32[]{:S(2)}) async-start(), calls=%async_computation.21 | async-start | bytes 737280 | tf_op jit(solution)/shard_map/reduce_scatter | solution.py:246
  373.2 166.3 %reduce-scatter.26.cloned.1.call-start = ((), (), s32[]{:S(2)}) async-start(), calls=%async_computation.22 | async-start | bytes 737280 | tf_op jit(solution)/shard_map/reduce_scatter | solution.py:247
  374.6 251.4 %all-reduce.14.cloned.1.call-start = ((), (), s32[]{:S(2)}) async-start(), calls=%async_computation.32 | async-start | bytes 2621440 | tf_op jit(solution)/shard_map/psum | solution.py:26
  407.6 286.5 %reduce-scatter.28.cloned.1.call-start = ((), (), s32[]{:S(2)}) async-start(), calls=%async_computation.23 | async-start | bytes 1474560 | tf_op jit(solution)/shard_map/reduce_scatter | solution.py:248
  409.3 352.9 %reduce-scatter.30.cloned.1.call-start = ((), (), s32[]{:S(2)}) async-start(), calls=%async_computation.24 | async-start | bytes 1474560 | tf_op jit(solution)/shard_map/reduce_scatter | solution.py:249
  411.0 63.1 %copy-start.65 = (f32[80,256]{1,0:T(8,128)S(1)}, f32[80,256]{1,0:T(8,128)}, u32[]{:S(2)}) copy-start(f32[80,256]{1,0:T(8,128)} %param.44) | copy-start | bytes 245764
  411.0 419.3 %reduce-scatter.32.cloned.1.call-start = ((), (), s32[]{:S(2)}) async-start(), calls=%async_computation.25 | async-start | bytes 1474560 | tf_op jit(solution)/shard_map/reduce_scatter | solution.py:250
  412.7 126.8 %copy-start.66 = (f32[80,256]{1,0:T(8,128)S(1)}, f32[80,256]{1,0:T(8,128)}, u32[]{:S(2)}) copy-start(f32[80,256]{1,0:T(8,128)} %param.47) | copy-start | bytes 245764
  412.7 213.3 %copy-start.63 = (f32[80,256]{1,0:T(8,128)S(1)}, f32[80,256]{1,0:T(8,128)}, u32[]{:S(2)}) copy-start(f32[80,256]{1,0:T(8,128)} %param.46) | copy-start | bytes 245764
  412.7 213.3 %copy-start.64 = (f32[80,256]{1,0:T(8,128)S(1)}, f32[80,256]{1,0:T(8,128)}, u32[]{:S(2)}) copy-start(f32[80,256]{1,0:T(8,128)} %param.45) | copy-start | bytes 245764
  412.7 281.4 %copy-start.60 = (f32[80,512]{1,0:T(8,128)S(1)}, f32[80,512]{1,0:T(8,128)}, u32[]{:S(2)}) copy-start(f32[80,512]{1,0:T(8,128)} %param.48) | copy-start | bytes 491524
  475.6 286.6 %copy-start.61 = (f32[80,512]{1,0:T(8,128)S(1)}, f32[80,512]{1,0:T(8,128)}, u32[]{:S(2)}) copy-start(f32[80,512]{1,0:T(8,128)} %param.49) | copy-start | bytes 491524
  476.5 353.8 %copy-start.62 = (f32[80,512]{1,0:T(8,128)S(1)}, f32[80,512]{1,0:T(8,128)}, u32[]{:S(2)}) copy-start(f32[80,512]{1,0:T(8,128)} %param.50) | copy-start | bytes 491524
  832.0 19.1 %all-to-all-start = ((bf16[8,80,512]{2,1,0:T(8,128)(2,1)}), bf16[8,80,512]{2,1,0:T(8,128)(2,1)S(1)}, u32[]{:S(2)}, u32[]{:S(2)}) async-start(bf16[8,80,512]{2,1,0:T(8,128)(2,1)} %get-tuple-element.130), calls=%async_computation.9 | async-start | bytes 1310720 | tf_op jit(solution)/shard_map/all_to_all | solution.py:273
  835.5 39.8 %reduce-scatter.34.cloned.1.call-start = ((), (), s32[]{:S(2)}) async-start(), calls=%async_computation.26 | async-start | bytes 1024000 | tf_op jit(solution)/shard_map/reduce_scatter | solution.py:73
  852.7 63.9 %reduce-scatter.36.cloned.1.call-start = ((), (), s32[]{:S(2)}) async-start(), calls=%async_computation.27 | async-start | bytes 1024000 | tf_op jit(solution)/shard_map/reduce_scatter | solution.py:73
  892.5 59.9 %reduce-scatter.38.cloned.1.call-start = ((), (), s32[]{:S(2)}) async-start(), calls=%async_computation.28 | async-start | bytes 1024000 | tf_op jit(solution)/shard_map/reduce_scatter | solution.py:73
  928.3 59.7 %reduce-scatter.40.cloned.1.call-start = ((), (), s32[]{:S(2)}) async-start(), calls=%async_computation.29 | async-start | bytes 1024000 | tf_op jit(solution)/shard_map/reduce_scatter | solution.py:73
  963.9 59.7 %reduce-scatter.42.cloned.1.call-start = ((), (), s32[]{:S(2)}) async-start(), calls=%async_computation.30 | async-start | bytes 1024000 | tf_op jit(solution)/shard_map/reduce_scatter | solution.py:73
  999.5 48.9 %reduce-scatter.22.cloned.1.call-start = ((), (), s32[]{:S(2)}) async-start(), calls=%async_computation.20 | async-start | bytes 819200 | tf_op jit(solution)/shard_map/reduce_scatter | solution.py:63
  1002.8 71.5 %reduce-scatter.44.cloned.1.call-start = ((), (), s32[]{:S(2)}) async-start(), calls=%async_computation.31 | async-start | bytes 1024000 | tf_op jit(solution)/shard_map/reduce_scatter | solution.py:73
  1085.0 55.2 %copy-start.15 = (f32[128,640]{1,0:T(8,128)S(1)}, f32[128,640]{1,0:T(8,128)}, u32[]{:S(2)}) copy-start(f32[128,640]{1,0:T(8,128)} %copy-done.14) | copy-start | bytes 983044
  1085.1 56.0 %copy-start.47 = (f32[80,512]{1,0:T(8,128)S(1)}, f32[80,512]{1,0:T(8,128)}, u32[]{:S(2)}) copy-start(f32[80,512]{1,0:T(8,128)} %param.41) | copy-start | bytes 491524
  1085.1 56.0 %copy-start.48 = (f32[80,512]{1,0:T(8,128)S(1)}, f32[80,512]{1,0:T(8,128)}, u32[]{:S(2)}) copy-start(f32[80,512]{1,0:T(8,128)} %param.42) | copy-start | bytes 491524
  1085.1 56.0 %copy-start.49 = (f32[80,512]{1,0:T(8,128)S(1)}, f32[80,512]{1,0:T(8,128)}, u32[]{:S(2)}) copy-start(f32[80,512]{1,0:T(8,128)} %param.43) | copy-start | bytes 491524
  1085.1 55.9 %all-to-all-start.1 = ((bf16[8,80,512]{2,1,0:T(8,128)(2,1)}), bf16[8,80,512]{2,1,0:T(8,128)(2,1)S(1)}, u32[]{:S(2)}, u32[]{:S(2)}) async-start(bf16[8,80,512]{2,1,0:T(8,128)(2,1)} %bitcast.48), calls=%async_computation.16 | async-start | bytes 1310720 | tf_op jit(solution)/shard_map/all_to_all | solution.py:284
  (66 other events, 742.0 us)
Sparse Core Ops, SparseCore 0:
  154.6 22.7 reduce-scatter.15
  274.3 22.8 reduce-scatter.17
  314.0 22.9 reduce-scatter.19
  367.9 39.6 all-reduce.15
  411.3 62.7 reduce-scatter.23
  477.8 61.7 reduce-scatter.25
  543.2 82.7 all-reduce.13
  629.9 64.1 reduce-scatter.27
  698.1 64.1 reduce-scatter.29
  766.1 64.1 reduce-scatter.31
  852.8 22.4 reduce-scatter.33
  892.6 23.9 reduce-scatter.35
  928.4 23.9 reduce-scatter.37
  964.0 23.9 reduce-scatter.39
  999.6 23.9 reduce-scatter.41
  1026.0 22.3 reduce-scatter.21
  1050.8 23.4 reduce-scatter.43
